TPU v7x, 128 devices: a whole 4x4x4 slice. The times are simulated.
128 devices in a mesh: blk: 32 (over x, y, core), mp: 4 (over z).
Axes of the slice: x: 4, y: 4, z: 4, core: 2. Of those that a mesh axis runs over, the one named last changes fastest.
Arguments:
- hidden: bfloat16 [144, 3584], replicated, may hold values from -6 to 6
- medusa_w: bfloat16 [2, 3584, 3584], P(None, 'blk', 'mp'), may hold values from -0.09375 to 0.09375
- embedding: bfloat16 [131072, 3584], P(('blk', 'mp')), may hold values from -0.5 to 0.5
- cand_ids: int32 [2, 144, 10], replicated, may hold values from 0 to 131071
- tree_q: bfloat16 [12, 48, 4096], P(None, None, 'mp'), may hold values from -6 to 6
- tree_key_value: bfloat16 [2, 12, 48, 2048], P(None, None, None, 'mp'), may hold values from -6 to 6
- prompt_key_value: bfloat16 [2, 32, 2048, 2048], P(None, 'blk', None, 'mp'), may hold values from -6 to 6
- block_group: int32 [32], P('blk'), may hold values from 0 to 11, as said below
- block_len: int32 [32], P('blk'), may hold values from 1 to 2048
- block_empty: int32 [32], P('blk'), may hold values 0 or 1
- parents: int32 [12, 48], replicated, may hold values from 0 to 46, as said below
- out_weight: bfloat16 [4096, 3584], P('mp'), may hold values from -0.09375 to 0.09375
- post_gain: float32 [3584], replicated, may hold values from 0.5 to 1.5
- resid: bfloat16 [576, 3584], P('blk'), may hold values from -6 to 6
Outputs:
- draft_logprob: float32 [2, 144, 10], replicated
- layer_out: bfloat16 [576, 3584], P('blk')
Inputs may be any that keep to these rules, and one draw needn't show every extreme that they name: `block_group`: every group number from 0 to min(12, 32) - 1 owns at least one block. `parents`: entry 0 of each row is 0; entry i for i >= 1 is below i; some group's last token has parent 48 - 2.
All inputs are finite; a program needn't handle non-finite values. No bound on the sum of `block_empty` on one device may be relied on, other than what follows from the above.
Results may differ from a plain program's by a relative error of at most 0.005.
Values may be sent and summed in bfloat16 or wider, within the bound.
A program may use at most 128 MiB of HBM per device.

v0:
```python
import jax
import jax.numpy as jnp
from jax import lax
from jax.sharding import PartitionSpec as P

HEAD_SIZE = 256


def capped(values, limit):
    return limit * jnp.tanh(values / limit)


def ancestry(parents):
    count = parents.shape[1]
    column = jnp.arange(count, dtype=jnp.int32)
    linked = (parents[:, :, None] == column[None, None, :]) & (column[None, :, None] > 0)
    reach = jnp.eye(count, dtype=jnp.float32)[None] + linked.astype(jnp.float32)
    for sweep in range(count.bit_length()):
        reach = jnp.minimum(
            jnp.einsum("gij,gjk->gik", reach, reach, precision=lax.Precision.HIGHEST), 1.0
        )
    return reach


def attend(queries, keys, values, mask):
    rows = queries.shape[0]
    length = keys.shape[0]
    kv_heads = keys.shape[1] // HEAD_SIZE
    repeats = queries.shape[1] // keys.shape[1]
    query_view = queries.reshape(rows, kv_heads, repeats, HEAD_SIZE)
    key_view = keys.reshape(length, kv_heads, HEAD_SIZE)
    value_view = values.reshape(length, kv_heads, HEAD_SIZE)
    scores = jnp.einsum(
        "qhrd,khd->hrqk", query_view, key_view, preferred_element_type=jnp.float32
    ) * HEAD_SIZE ** (-0.5)
    weights = jnp.exp(capped(scores, 50.0)) * mask[None, None]
    denominator = jnp.sum(weights, -1).transpose(2, 0, 1).reshape(rows, kv_heads * repeats)
    numerator = jnp.einsum(
        "hrqk,khd->qhrd",
        weights.astype(jnp.bfloat16),
        value_view,
        preferred_element_type=jnp.float32,
    )
    return (numerator.reshape(rows, kv_heads * repeats * HEAD_SIZE), denominator)


def per_device(
    hidden,
    medusa_w,
    embedding,
    cand_ids,
    tree_q,
    tree_key_value,
    prompt_key_value,
    block_group,
    block_len,
    block_empty,
    parents,
    out_weight,
    post_gain,
    resid,
):
    units = medusa_w.shape[2]
    inner = jnp.einsum(
        "rd,mdu->mru",
        hidden,
        lax.all_gather(medusa_w, "blk", axis=1, tiled=True),
        preferred_element_type=jnp.float32,
    )
    own_cols = lax.dynamic_slice_in_dim(hidden, lax.axis_index("mp") * units, units, 1).astype(
        jnp.float32
    )
    fresh = (own_cols[None] + jax.nn.silu(inner)).astype(jnp.bfloat16)
    full_fresh = lax.all_gather(fresh, "mp", axis=2, tiled=True)
    logits = capped(
        jnp.einsum("mrd,vd->mrv", full_fresh, embedding, preferred_element_type=jnp.float32), 30.0
    )
    totals = jnp.sum(jnp.exp(logits), -1)
    vocab_dev = embedding.shape[0]
    first_id = lax.axis_index(("blk", "mp")) * vocab_dev
    local_ids = cand_ids - first_id
    match = local_ids[..., None] == jnp.arange(vocab_dev, dtype=jnp.int32)
    picked = jnp.sum(jnp.where(match, logits[:, :, None, :], 0.0), -1)
    totals, picked = lax.psum((totals, picked), ("blk", "mp"))
    draft_logprob = picked - jnp.log(totals)[..., None]
    groups, tree_size, features = tree_q.shape
    keys = prompt_key_value[0, 0]
    values = prompt_key_value[1, 0]
    length = keys.shape[0]
    group = block_group[0]
    key_ok = ((jnp.arange(length, dtype=jnp.int32) < block_len[0]) & (block_empty[0] == 0)).astype(
        jnp.float32
    )
    row_group = jnp.arange(groups * tree_size, dtype=jnp.int32) // tree_size
    mask = (row_group == group).astype(jnp.float32)[:, None] * key_ok[None, :]
    numer, denom = attend(tree_q.reshape(groups * tree_size, features), keys, values, mask)
    rows_dev = groups * tree_size // lax.axis_size("blk")
    first_row = lax.axis_index("blk") * rows_dev
    summed = lax.psum((numer, denom), "blk")
    numer = lax.dynamic_slice_in_dim(summed[0], first_row, rows_dev, 0)
    denom = lax.dynamic_slice_in_dim(summed[1], first_row, rows_dev, 0)
    reach = ancestry(parents)
    tree_numer, tree_denom = jax.vmap(attend)(tree_q, tree_key_value[0], tree_key_value[1], reach)
    heads_dev = tree_denom.shape[2]
    tree_numer = lax.dynamic_slice_in_dim(
        tree_numer.reshape(groups * tree_size, features), first_row, rows_dev, 0
    )
    tree_denom = lax.dynamic_slice_in_dim(
        tree_denom.reshape(groups * tree_size, heads_dev), first_row, rows_dev, 0
    )
    numer = numer + tree_numer
    denom = denom + tree_denom
    heads_out = (
        (numer.reshape(rows_dev, heads_dev, HEAD_SIZE) / denom[..., None])
        .reshape(rows_dev, features)
        .astype(jnp.bfloat16)
    )
    attn = lax.psum(jnp.dot(heads_out, out_weight, preferred_element_type=jnp.float32), "mp")
    normed = attn * lax.rsqrt(jnp.mean(attn * attn, -1, keepdims=True) + 1e-06) * post_gain
    layer_out = (normed + resid.astype(jnp.float32)).astype(jnp.bfloat16)
    return (draft_logprob, layer_out)


def solution(mesh):
    placed = (
        P(),
        P(None, "blk", "mp"),
        P(("blk", "mp"), None),
        P(),
        P(None, None, "mp"),
        P(None, None, None, "mp"),
        P(None, "blk", None, "mp"),
        P("blk"),
        P("blk"),
        P("blk"),
        P(),
        P("mp", None),
        P(),
        P("blk", None),
    )
    return jax.shard_map(
        per_device, mesh=mesh, in_specs=placed, out_specs=(P(), P("blk", None)), check_vma=False
    )
```

profile of v0, /device:TPU:1, one launch (start us, length us, event | category | flops | bytes accessed | tf_op | source)
XLA Modules:
  0.0 381.7 jit_solution(4261685247920140671)
XLA Ops:
  7.2 0.0 all-reduce.4.cloned.1.call-start
  7.2 4.4 %fusion.51 = (bf16[1,1,2048,512]{3,2,1,0:T(8,128)(2,1)}, bf16[1,1,2048,512]{3,2,1,0:T(8,128)(2,1)}) fusion(bf16[2,1,2048,512]{3,2,1,0:T(8,128)(2,1)} %param.20), kind=kLoop, calls=%fused_computation.70 | loop fusion | bytes 8388608 | tf_op jit(solution)/shard_map/slice | solution.py:88
  11.6 2.9 copy.79
  16.5 3.3 reshape_reshape.3
  19.8 4.0 %copy.80 = bf16[1,1,2048,512]{2,3,1,0:T(8,128)(2,1)} copy(bf16[1,1,2048,512]{3,2,1,0:T(8,128)(2,1)} %get-tuple-element.6) | data formatting | bytes 4194304
  23.8 0.4 broadcast_multiply_fusion
  24.2 0.0 copy-start.1
  24.2 10.5 %fusion = (f32[2,2,576]{2,1,0:T(2,128)}, f32[2,2048,576,2]{1,2,3,0:T(8,128)}) fusion(f32[576,2048]{1,0:T(8,128)S(1)} %broadcast_multiply_fusion, bf16[2048,2,256,1]{0,2,3,1:T(8,128)(2,1)S(1)} %bitcast.83, bf16[576,2,2,256]{3,2,1,0:T(2,128)(2,1)S(1)} %reshape_reshape.3), kind=kOutput, calls=%fused_computation.1 | convolution fusion | flops 2434791168 | bytes 26878976 | tf_op jit(solution)/shard_map/qhrd,khd->hrqk/dot_general | solution.py:33
  34.7 0.0 copy-done.1
  34.7 9.1 %fusion.6 = f32[576,2,2,256]{3,0,2,1:T(8,128)S(1)} fusion(bf16[2048,2,256,1]{0,2,3,1:T(8,128)(2,1)S(1)} %bitcast.85, f32[2,2048,576,2]{1,2,3,0:T(8,128)} %get-tuple-element.15, f32[576,2048]{1,0:T(8,128)S(1)} %broadcast_multiply_fusion), kind=kOutput, calls=%fused_computation.10 | convolution fusion | flops 2434793472 | bytes 28049408 | tf_op jit(solution)/shard_map/hrqk,khd->qhrd/dot_general | solution.py:38
  43.8 1.8 copy.56
  45.6 2.9 reshape.101
  48.6 0.0 copy-start
  48.6 0.0 copy-start.2
  48.6 0.0 all-reduce.4.cloned.1.call-update
  48.6 0.0 all-gather.3.cloned.1.call-start
  48.6 0.7 all-gather.3.cloned.1.call-update
  49.3 0.2 all-reduce.6.cloned.1.call-start
  49.6 0.3 copy-done
  49.8 0.9 reshape.102
  50.7 0.7 reshape.104
  51.4 0.0 copy-done.2
  51.4 0.1 fusion.52
  51.5 0.1 reshape_squeeze.14
  51.7 1.4 convolution_minimum_fusion.5
  53.1 0.4 convolution_minimum_fusion.4
  53.5 0.4 convolution_minimum_fusion.3
  53.9 0.4 convolution_minimum_fusion.2
  54.4 0.4 convolution_minimum_fusion.1
  54.8 0.4 convolution_minimum_fusion
  55.2 0.1 copy.59
  55.3 0.9 fusion.53
  56.2 0.1 reshape.105
  56.3 124.9 %psum.38 = f32[576,4]{0,1:T(4,128)S(1)} all-reduce(f32[576,4]{0,1:T(4,128)S(1)} %reshape.104), channel_id=1, replica_groups=mesh['blk'=32,'mp'=4] {'blk'}, use_global_device_ids=true, to_apply=%region_6.7 | all-reduce | flops 2304 | bytes 18432 | tf_op jit(solution)/shard_map/psum | solution.py:99
  181.2 0.1 dynamic-slice_add_fusion
  181.3 0.1 copy.64
  181.4 0.1 div.48
  181.5 0.1 reshape_squeeze.15
  181.7 0.5 convolution_bitcast_fusion
  182.2 1.8 copy.62
  184.0 0.0 copy-start.4
  184.1 2.9 reshape.103
  187.0 0.0 copy-done.4
  187.0 0.0 all-reduce.4.cloned.1.call-done
  187.1 5.1 %fusion.39 = f32[18,3584]{1,0:T(8,128)} fusion(bf16[1024,3584]{1,0:T(8,128)(2,1)} %param.25, f32[18,1024]{1,0:T(8,128)S(1)} %bitcast.87, f32[576,1024]{1,0:T(8,128)} %reshape.103, s32[]{:T(128)S(6)} %select_n.25, f32[576,1024]{1,0:T(8,128)} %all-reduce.4.cloned.1.call-done), kind=kOutput, calls=%fused_computation.47 | convolution fusion | flops 132175872 | bytes 7868420 | tf_op jit(solution)/shard_map/dot_general | solution.py:118
  192.1 0.0 all-reduce.6.cloned.1.call-update
  192.1 0.0 copy-start.5
  192.2 0.0 copy-start.3
  192.2 0.0 copy-start.6
  192.2 0.3 all-gather.5.cloned.1.call-start
  192.4 32.7 %all-gather.3.cloned.1.call-done = bf16[2,3584,896]{2,1,0:T(8,128)(2,1)} async-done(((bf16[2,112,896]{2,1,0:T(8,128)(2,1)}), bf16[2,3584,896]{2,1,0:T(8,128)(2,1)}) %all-gather.3.cloned.1.call-update) | async-done | bytes 12845072 | tf_op jit(solution)/shard_map/all_gather | solution.py:67
  225.2 7.6 %add_convert_fusion = bf16[2,144,896]{2,1,0:T(8,128)(2,1)} fusion(bf16[2,3584,896]{2,1,0:T(8,128)(2,1)} %all-gather.3.cloned.1.call-done, bf16[144,3584]{1,0:T(8,128)(2,1)S(1)} %copy-done.4, f32[144,896]{1,0:T(8,128)S(1)} %dynamic-slice_convert_fusion), kind=kOutput, calls=%fused_computation.32 | convolution fusion | flops 1851236352 | bytes 14909440 | tf_op jit(solution)/shard_map/rd,mdu->mru/dot_general | solution.py:64
  232.8 0.0 all-gather.5.cloned.1.call-update
  232.8 0.0 copy-done.5
  232.8 34.1 %all-reduce.6.cloned.1.call-done = f32[18,3584]{1,0:T(8,128)} async-done(((f32[18,3584]{1,0:T(8,128)}), f32[18,3584]{1,0:T(8,128)}) %all-reduce.6.cloned.1.call-update) | async-done | bytes 258064 | tf_op jit(solution)/shard_map/psum | solution.py:118
  266.9 1.1 multiply_reduce_fusion
  268.0 0.0 copy-done.3
  268.0 0.0 copy-done.6
  268.0 1.8 add_convert_fusion.1
  269.8 31.7 %all-gather.5.cloned.1.call-done = bf16[2,144,3584]{2,1,0:T(8,128)(2,1)} async-done(((bf16[2,144,896]{2,1,0:T(8,128)(2,1)}), bf16[2,144,3584]{2,1,0:T(8,128)(2,1)}) %all-gather.5.cloned.1.call-update) | async-done | bytes 2064400 | tf_op jit(solution)/shard_map/all_gather | solution.py:74
  301.5 6.2 %exponential_reduce_fusion = (f32[2,144]{1,0:T(2,128)S(1)}, f32[2,144,1024]{2,1,0:T(8,128)S(1)}) fusion(bf16[2,144,3584]{2,1,0:T(8,128)(2,1)} %all-gather.5.cloned.1.call-done, bf16[1024,3584]{1,0:T(8,128)(2,1)} %param.16), kind=kOutput, calls=%fused_computation.24 | convolution fusion | flops 2114813696 | bytes 10585216 | tf_op jit(solution)/shard_map/mrd,vd->mrv/dot_general | solution.py:76
  307.8 1.8 select_reduce_fusion
  309.6 64.9 %all-reduce = (f32[2,144,10]{1,2,0:T(8,128)S(1)}, f32[2,144]{1,0:T(2,128)S(1)}) all-reduce(f32[2,144,10]{1,2,0:T(8,128)S(1)} %select_reduce_fusion, f32[2,144]{1,0:T(2,128)S(1)} %get-tuple-element.10), channel_id=1, replica_groups=mesh['blk'=32,'mp'=4] {'blk','mp'}, use_global_device_ids=true, to_apply=%region_1.2 | all-reduce | flops 3168 | bytes 25344 | tf_op jit(solution)/shard_map/psum | solution.py:84
  374.5 0.6 copy.65
  (13 shorter events, 0.1 us)
Async XLA Ops:
  7.2 179.9 %all-reduce.4.cloned.1.call-start = ((), (), s32[]{:S(2)}) async-start(), calls=%async_computation.2 | async-start | bytes 4718592 | tf_op jit(solution)/shard_map/psum | solution.py:99
  24.2 10.5 %copy-start.1 = (bf16[1,1,2048,512]{2,3,1,0:T(8,128)(2,1)S(1)}, bf16[1,1,2048,512]{2,3,1,0:T(8,128)(2,1)}, u32[]{:S(2)}) copy-start(bf16[1,1,2048,512]{2,3,1,0:T(8,128)(2,1)} %copy.80) | copy-start | bytes 6291460
  48.6 1.3 copy-start
  48.6 2.9 copy-start.2
  48.6 176.6 %all-gather.3.cloned.1.call-start = ((), (), s32[]{:S(2)}) async-start(), calls=%async_computation | async-start | bytes 13246464 | tf_op jit(solution)/shard_map/all_gather | solution.py:67
  49.3 217.6 %all-reduce.6.cloned.1.call-start = ((), (), s32[]{:S(2)}) async-start(), calls=%async_computation.3 | async-start | bytes 688128 | tf_op jit(solution)/shard_map/psum | solution.py:118
  184.0 3.0 copy-start.4
  192.1 40.7 %copy-start.5 = (s32[2,144,10]{1,0,2:T(2,128)S(1)}, s32[2,144,10]{1,0,2:T(2,128)}, u32[]{:S(2)}) copy-start(s32[2,144,10]{1,0,2:T(2,128)} %param.17) | copy-start | bytes 34564
  192.2 75.9 %copy-start.3 = (bf16[18,3584]{1,0:T(8,128)(2,1)S(1)}, bf16[18,3584]{1,0:T(8,128)(2,1)}, u32[]{:S(2)}) copy-start(bf16[18,3584]{1,0:T(8,128)(2,1)} %param.27) | copy-start | bytes 387076
  192.2 75.9 %copy-start.6 = (f32[3584]{0:T(1024)S(1)}, f32[3584]{0:T(1024)}, u32[]{:S(2)}) copy-start(f32[3584]{0:T(1024)} %param.26) | copy-start | bytes 43012
  192.2 109.4 %all-gather.5.cloned.1.call-start = ((), (), s32[]{:S(2)}) async-start(), calls=%async_computation.1 | async-start | bytes 2580480 | tf_op jit(solution)/shard_map/all_gather | solution.py:74
Sparse Core Ops, SparseCore 0:
  48.7 110.4 all-reduce.3
  161.6 63.5 all-gather.2
  227.5 39.3 all-reduce.5
  268.4 33.0 all-gather.4
where the time goes:
time: 382 us
  blocking collectives  190 us (50%)
  waiting for transfers between devices  99.3 us (26%)
  matrix products  43.3 us (11%)
  local copies, waits for them, and re-layouts  27.5 us (7%)
  between operations  16 us (4%)
  other arithmetic  5.25 us (1%)
    psum x1, blocking collectives, per_device(): summed = lax.psum((numer, denom), 'blk')  125 us
    psum x1, blocking collectives, per_device(): totals, picked = lax.psum((totals, picked), ('blk', 'mp'))  64.9 us
    psum x1, waiting for transfers between devices, per_device(): lax.psum(jnp.dot(heads_out, out_weight, preferred_element_type=jnp.float3...  34.1 us
    all_gather x1, waiting for transfers between devices, per_device(): lax.all_gather(medusa_w, 'blk', axis=1, tiled=True)  32.7 us
    all_gather x1, waiting for transfers between devices, per_device(): full_fresh = lax.all_gather(fresh, 'mp', axis=2, tiled=True)  31.7 us
    dot_general x2, matrix products, attend(): jnp.einsum('qhrd,khd->hrqk', query_view, key_view, preferred_element_type...  11.3 us
    dot_general x2, matrix products, attend(): jnp.einsum('hrqk,khd->qhrd', weights.astype(jnp.bfloat16), value_view, pr...  9.63 us
    unnamed x19, local copies, waits for them, and re-layouts  7.84 us
  transfers between devices with their start and end apart: 4, of which 3 were waited for; matrix products, arithmetic and copies ran while one was open for 7% of the time, Pallas kernels for 0%

commit v1 on v0

--- a/solution.py
+++ b/solution.py
@@ -71,7 +71,19 @@
         jnp.float32
     )
     fresh = (own_cols[None] + jax.nn.silu(inner)).astype(jnp.bfloat16)
-    full_fresh = lax.all_gather(fresh, "mp", axis=2, tiled=True)
+    ways, here, hop = (lax.axis_size("mp"), lax.axis_index("mp"), fresh.shape[2])
+    shape = [n * ways if d == 2 else n for d, n in enumerate(fresh.shape)]
+    full = lax.dynamic_update_slice_in_dim(jnp.zeros(shape, fresh.dtype), fresh, here * hop, axis=2)
+    going_up = going_down = fresh
+    for far in range(1, ways // 2 + 1):
+        going_up = lax.ppermute(going_up, "mp", [(d, (d + 1) % ways) for d in range(ways)])
+        full = lax.dynamic_update_slice_in_dim(full, going_up, (here - far) % ways * hop, axis=2)
+        if 2 * far < ways:
+            going_down = lax.ppermute(going_down, "mp", [(d, (d - 1) % ways) for d in range(ways)])
+            full = lax.dynamic_update_slice_in_dim(
+                full, going_down, (here + far) % ways * hop, axis=2
+            )
+    full_fresh = full
     logits = capped(
         jnp.einsum("mrd,vd->mrv", full_fresh, embedding, preferred_element_type=jnp.float32), 30.0
     )

time: 382 us -> 365 us (0.955)
  waiting for transfers between devices: 99.3 us -> 76.3 us
    all_gather x1 -> x0, waiting for transfers between devices: 31.7 us -> none  [per_device(): full_fresh = lax.all_gather(fresh, 'mp', axis=2, tiled=True)]
    ppermute x0 -> x3, waiting for transfers between devices: none -> 9.6 us  [the longest x1 7.08 us: per_device(): lax.ppermute(going_down, 'mp', [(d, (d - 1) % ways) for d in range(ways)])]
    unnamed x19 -> x17, local copies, waits for them, and re-layouts: 7.84 us -> 7.78 us
  transfers between devices with their start and end apart: 4 -> 6, of which waited for: 3 -> 4; matrix products, arithmetic and copies ran while one was open for 7% -> 8% of each run, Pallas kernels for 0% -> 0%
where the time goes in v1:
time: 365 us
  blocking collectives  193 us (53%)
  waiting for transfers between devices  76.3 us (21%)
  matrix products  42.3 us (12%)
  local copies, waits for them, and re-layouts  27.7 us (8%)
  between operations  16.1 us (4%)
  other arithmetic  6.19 us (2%)
    psum x1, blocking collectives, per_device(): summed = lax.psum((numer, denom), 'blk')  125 us
    psum x1, blocking collectives, per_device(): totals, picked = lax.psum((totals, picked), ('blk', 'mp'))  68 us
    psum x1, waiting for transfers between devices, per_device(): lax.psum(jnp.dot(heads_out, out_weight, preferred_element_type=jnp.float3...  33.9 us
    all_gather x1, waiting for transfers between devices, per_device(): lax.all_gather(medusa_w, 'blk', axis=1, tiled=True)  32.1 us
    dot_general x2, matrix products, attend(): jnp.einsum('qhrd,khd->hrqk', query_view, key_view, preferred_element_type...  11.3 us
    dot_general x2, matrix products, attend(): jnp.einsum('hrqk,khd->qhrd', weights.astype(jnp.bfloat16), value_view, pr...  9.63 us
    unnamed x17, local copies, waits for them, and re-layouts  7.78 us
  transfers between devices with their start and end apart: 6, of which 4 were waited for; matrix products, arithmetic and copies ran while one was open for 8% of the time, Pallas kernels for 0%

profile of v1, /device:TPU:1, one launch (start us, length us, event | category | flops | bytes accessed | tf_op | source)
XLA Modules:
  0.0 364.7 jit_solution(16832484123569222972)
XLA Ops:
  7.2 0.0 all-reduce.4.cloned.1.call-start
  7.2 4.4 %fusion.52 = (bf16[1,1,2048,512]{3,2,1,0:T(8,128)(2,1)}, bf16[1,1,2048,512]{3,2,1,0:T(8,128)(2,1)}) fusion(bf16[2,1,2048,512]{3,2,1,0:T(8,128)(2,1)} %param.20), kind=kLoop, calls=%fused_computation.76 | loop fusion | bytes 8388608 | tf_op jit(solution)/shard_map/slice | solution.py:100
  11.6 2.9 copy.79
  16.5 3.3 reshape_reshape.3
  19.8 4.0 %copy.80 = bf16[1,1,2048,512]{2,3,1,0:T(8,128)(2,1)} copy(bf16[1,1,2048,512]{3,2,1,0:T(8,128)(2,1)} %get-tuple-element.6) | data formatting | bytes 4194304
  23.8 0.4 broadcast_multiply_fusion
  24.2 0.0 copy-start.1
  24.2 10.5 %fusion = (f32[2,2,576]{2,1,0:T(2,128)}, f32[2,2048,576,2]{1,2,3,0:T(8,128)}) fusion(f32[576,2048]{1,0:T(8,128)S(1)} %broadcast_multiply_fusion, bf16[2048,2,256,1]{0,2,3,1:T(8,128)(2,1)S(1)} %bitcast.85, bf16[576,2,2,256]{3,2,1,0:T(2,128)(2,1)S(1)} %reshape_reshape.3), kind=kOutput, calls=%fused_computation.1 | convolution fusion | flops 2434791168 | bytes 26878976 | tf_op jit(solution)/shard_map/qhrd,khd->hrqk/dot_general | solution.py:33
  34.7 9.1 %fusion.6 = f32[576,2,2,256]{3,0,2,1:T(8,128)S(1)} fusion(bf16[2048,2,256,1]{0,2,3,1:T(8,128)(2,1)S(1)} %bitcast.87, f32[2,2048,576,2]{1,2,3,0:T(8,128)} %get-tuple-element.17, f32[576,2048]{1,0:T(8,128)S(1)} %broadcast_multiply_fusion), kind=kOutput, calls=%fused_computation.10 | convolution fusion | flops 2434793472 | bytes 28049408 | tf_op jit(solution)/shard_map/hrqk,khd->qhrd/dot_general | solution.py:38
  43.8 1.8 copy.56
  45.6 2.9 reshape.101
  48.6 0.0 all-reduce.4.cloned.1.call-update
  48.6 0.0 all-gather.2.cloned.1.call-start
  48.6 0.7 all-gather.2.cloned.1.call-update
  49.3 0.2 all-reduce.6.cloned.1.call-start
  49.6 0.2 copy-done
  49.8 0.9 reshape.102
  50.7 0.7 reshape.104
  51.5 0.1 fusion.53
  51.5 0.1 reshape_squeeze.14
  51.7 1.4 convolution_minimum_fusion.5
  53.1 0.4 convolution_minimum_fusion.4
  53.5 0.4 convolution_minimum_fusion.3
  53.9 0.4 convolution_minimum_fusion.2
  54.4 0.4 convolution_minimum_fusion.1
  54.8 0.4 convolution_minimum_fusion
  55.2 0.1 copy.59
  55.3 0.9 fusion.54
  56.2 0.1 reshape.105
  56.3 124.9 %psum.38 = f32[576,4]{0,1:T(4,128)S(1)} all-reduce(f32[576,4]{0,1:T(4,128)S(1)} %reshape.104), channel_id=1, replica_groups=mesh['blk'=32,'mp'=4] {'blk'}, use_global_device_ids=true, to_apply=%region_6.7 | all-reduce | flops 2304 | bytes 18432 | tf_op jit(solution)/shard_map/psum | solution.py:111
  181.2 0.1 fusion.49
  181.3 0.1 copy.64
  181.4 0.1 div.48
  181.5 0.1 reshape_squeeze.15
  181.7 0.5 convolution_bitcast_fusion
  182.2 1.8 copy.62
  184.0 2.9 reshape.103
  187.0 1.0 dynamic-slice_convert_fusion
  188.0 0.0 all-reduce.4.cloned.1.call-done
  188.0 5.1 %fusion.39 = f32[18,3584]{1,0:T(8,128)} fusion(bf16[1024,3584]{1,0:T(8,128)(2,1)} %param.25, f32[18,1024]{1,0:T(8,128)S(1)} %bitcast.89, f32[576,1024]{1,0:T(8,128)} %reshape.103, s32[]{:T(128)S(6)} %select_n.56, f32[576,1024]{1,0:T(8,128)} %all-reduce.4.cloned.1.call-done), kind=kOutput, calls=%fused_computation.47 | convolution fusion | flops 132175872 | bytes 7868420 | tf_op jit(solution)/shard_map/dot_general | solution.py:130
  193.0 0.0 all-reduce.6.cloned.1.call-update
  193.1 32.1 %all-gather.2.cloned.1.call-done = bf16[2,3584,896]{2,1,0:T(8,128)(2,1)} async-done(((bf16[2,112,896]{2,1,0:T(8,128)(2,1)}), bf16[2,3584,896]{2,1,0:T(8,128)(2,1)}) %all-gather.2.cloned.1.call-update) | async-done | bytes 12845072 | tf_op jit(solution)/shard_map/all_gather | solution.py:67
  225.2 0.1 broadcast_in_dim.14
  225.3 0.0 copy-start.4
  225.3 0.0 copy-start.3
  225.3 0.0 copy-start.5
  225.3 7.2 %constant_dynamic-update-slice_fusion.3 = (bf16[2,144,3584]{2,1,0:T(8,128)(2,1)S(1)}, bf16[2,144,896]{2,1,0:T(8,128)(2,1)S(1)}) fusion(bf16[2,144,3584]{2,1,0:T(8,128)(2,1)S(1)} %broadcast_in_dim.14, s32[]{:T(128)S(6)} %select_n.47, bf16[2,3584,896]{2,1,0:T(8,128)(2,1)} %all-gather.2.cloned.1.call-done, bf16[144,3584]{1,0:T(8,128)(2,1)} %param.14, ...), kind=kOutput, calls=%fused_computation.70 | convolution fusion | flops 1851236352 | bytes 15425540 | tf_op jit(solution)/shard_map/rd,mdu->mru/dot_general | solution.py:64
  232.5 1.3 collective-permute-start
  233.9 33.9 %all-reduce.6.cloned.1.call-done = f32[18,3584]{1,0:T(8,128)} async-done(((f32[18,3584]{1,0:T(8,128)}), f32[18,3584]{1,0:T(8,128)}) %all-reduce.6.cloned.1.call-update) | async-done | bytes 258064 | tf_op jit(solution)/shard_map/psum | solution.py:130
  267.8 1.1 multiply_reduce_fusion
  268.9 1.6 collective-permute-start.1
  270.5 0.0 collective-permute-done
  270.5 0.0 collective-permute-start.2
  270.5 0.0 copy-done.3
  270.5 1.8 add_convert_fusion.1
  272.3 0.1 constant_dynamic-update-slice_fusion.2
  272.4 7.1 %collective-permute-done.1 = bf16[2,144,896]{2,1,0:T(8,128)(2,1)S(1)} collective-permute-done((bf16[2,144,896]{2,1,0:T(8,128)(2,1)S(1)}, bf16[2,144,896]{2,1,0:T(8,128)(2,1)S(1)}, u32[]{:S(2)}, u32[]{:S(2)}) %collective-permute-start.1) | collective-permute-done | bytes 516128 | tf_op jit(solution)/shard_map/ppermute | solution.py:82
  279.4 0.1 constant_dynamic-update-slice_fusion.1
  279.5 2.5 collective-permute-done.2
  282.0 0.1 constant_dynamic-update-slice_fusion
  282.1 5.6 %exponential_reduce_fusion = (f32[2,144]{1,0:T(2,128)S(1)}, f32[2,144,1024]{2,1,0:T(8,128)S(1)}) fusion(bf16[2,144,3584]{2,1,0:T(8,128)(2,1)S(1)} %constant_dynamic-update-slice_fusion, bf16[1024,3584]{1,0:T(8,128)(2,1)} %param.16), kind=kOutput, calls=%fused_computation.24 | convolution fusion | flops 2114813696 | bytes 10585216 | tf_op jit(solution)/shard_map/mrd,vd->mrv/dot_general | solution.py:88
  287.7 1.8 select_reduce_fusion
  289.5 68.0 %all-reduce = (f32[2,144,10]{1,2,0:T(8,128)S(1)}, f32[2,144]{1,0:T(2,128)S(1)}) all-reduce(f32[2,144,10]{1,2,0:T(8,128)S(1)} %select_reduce_fusion, f32[2,144]{1,0:T(2,128)S(1)} %get-tuple-element.12), channel_id=1, replica_groups=mesh['blk'=32,'mp'=4] {'blk','mp'}, use_global_device_ids=true, to_apply=%region_1.2 | all-reduce | flops 3168 | bytes 25344 | tf_op jit(solution)/shard_map/psum | solution.py:96
  357.5 0.6 copy.65
  (18 shorter events, 0.1 us)
Async XLA Ops:
  7.2 180.8 %all-reduce.4.cloned.1.call-start = ((), (), s32[]{:S(2)}) async-start(), calls=%async_computation.1 | async-start | bytes 4718592 | tf_op jit(solution)/shard_map/psum | solution.py:111
  24.2 10.5 %copy-start.1 = (bf16[1,1,2048,512]{2,3,1,0:T(8,128)(2,1)S(1)}, bf16[1,1,2048,512]{2,3,1,0:T(8,128)(2,1)}, u32[]{:S(2)}) copy-start(bf16[1,1,2048,512]{2,3,1,0:T(8,128)(2,1)} %copy.80) | copy-start | bytes 6291460
  48.6 1.3 copy-start
  48.6 2.9 copy-start.2
  48.6 176.6 %all-gather.2.cloned.1.call-start = ((), (), s32[]{:S(2)}) async-start(), calls=%async_computation | async-start | bytes 13246464 | tf_op jit(solution)/shard_map/all_gather | solution.py:67
  49.3 218.5 %all-reduce.6.cloned.1.call-start = ((), (), s32[]{:S(2)}) async-start(), calls=%async_computation.2 | async-start | bytes 688128 | tf_op jit(solution)/shard_map/psum | solution.py:130
  225.3 8.6 %copy-start.4 = (s32[2,144,10]{1,0,2:T(2,128)S(1)}, s32[2,144,10]{1,0,2:T(2,128)}, u32[]{:S(2)}) copy-start(s32[2,144,10]{1,0,2:T(2,128)} %param.17) | copy-start | bytes 34564
  225.3 45.2 %copy-start.3 = (bf16[18,3584]{1,0:T(8,128)(2,1)S(1)}, bf16[18,3584]{1,0:T(8,128)(2,1)}, u32[]{:S(2)}) copy-start(bf16[18,3584]{1,0:T(8,128)(2,1)} %param.27) | copy-start | bytes 387076
  225.3 45.2 %copy-start.5 = (f32[3584]{0:T(1024)S(1)}, f32[3584]{0:T(1024)}, u32[]{:S(2)}) copy-start(f32[3584]{0:T(1024)} %param.26) | copy-start | bytes 43012
  232.5 38.0 %collective-permute-start = (bf16[2,144,896]{2,1,0:T(8,128)(2,1)S(1)}, bf16[2,144,896]{2,1,0:T(8,128)(2,1)S(1)}, u32[]{:S(2)}, u32[]{:S(2)}) collective-permute-start(bf16[2,144,896]{2,1,0:T(8,128)(2,1)S(1)} %get-tuple-element.11), channel_id=1, source_target_pairs={{0,1},{1,2},{2,3},{3,0},{4,5},{5,6},{6,7},{7,4},{8,9},{9,10},{10,1... | collective-permute-start | bytes 1548296 | tf_op jit(solution)/shard_map/ppermute | solution.py:79
  268.9 10.5 %collective-permute-start.1 = (bf16[2,144,896]{2,1,0:T(8,128)(2,1)S(1)}, bf16[2,144,896]{2,1,0:T(8,128)(2,1)S(1)}, u32[]{:S(2)}, u32[]{:S(2)}) collective-permute-start(bf16[2,144,896]{2,1,0:T(8,128)(2,1)S(1)} %get-tuple-element.11), channel_id=1, source_target_pairs={{0,3},{1,0},{2,1},{3,2},{4,7},{5,4},{6,5},{7,6},{8,11},{9,8},{10,9... | collective-permute-start | bytes 1548296 | tf_op jit(solution)/shard_map/ppermute | solution.py:82
  270.5 11.5 %collective-permute-start.2 = (bf16[2,144,896]{2,1,0:T(8,128)(2,1)S(1)}, bf16[2,144,896]{2,1,0:T(8,128)(2,1)S(1)}, u32[]{:S(2)}, u32[]{:S(2)}) collective-permute-start(bf16[2,144,896]{2,1,0:T(8,128)(2,1)S(1)} %collective-permute-done), channel_id=1, source_target_pairs={{0,1},{1,2},{2,3},{3,0},{4,5},{5,6},{6,7},{7,4},{8,9},{9,10},{10,1... | collective-permute-start | bytes 1548296 | tf_op jit(solution)/shard_map/ppermute | solution.py:79
Sparse Core Ops, SparseCore 0:
  48.7 110.4 all-reduce.3
  161.6 63.5 all-gather.1
  227.5 40.2 all-reduce.5
